TPU v7x, 32 devices: a whole 2x2x4 slice. The times are simulated.
32 devices in a mesh: fsdp: 16 (over z, x, core), rep: 2 (over y).
Axes of the slice: x: 2, y: 2, z: 4, core: 2. Of those that a mesh axis runs over, the one named last changes fastest.
Arguments:
- layer_input: bfloat16 [128, 256, 768], P(('fsdp', 'rep')), may hold values from -6 to 6
- slot_valid: int32 [128, 256], P(('fsdp', 'rep')), may hold values from 0 to 1, as said below
- projections: bfloat16 [3, 768, 768], P(None, 'fsdp'), may hold values from -0.21875 to 0.21875
- out_weight: bfloat16 [768, 768], P('fsdp'), may hold values from -1.25 to 1.25
- vectors: bfloat16 [8, 768], P(None, 'fsdp'), may hold values from -2 to 2
- up_weight: bfloat16 [768, 3072], P('fsdp'), may hold values from -0.21875 to 0.21875
- up_bias: bfloat16 [3072], P('fsdp'), may hold values from -3 to 3
- down_weight: bfloat16 [3072, 768], P('fsdp'), may hold values from -0.109375 to 0.109375
- cotangent: bfloat16 [128, 256, 768], P(('fsdp', 'rep')), may hold values from -6 to 6
Outputs:
- output: bfloat16 [128, 256, 768], P(('fsdp', 'rep'))
- grad_input: bfloat16 [128, 256, 768], P(('fsdp', 'rep'))
- grad_projections: float32 [3, 768, 768], P(None, 'fsdp')
- grad_out_weight: float32 [768, 768], P('fsdp')
- grad_vectors: float32 [8, 768], P(None, 'fsdp')
- grad_up_weight: float32 [768, 3072], P('fsdp')
- grad_up_bias: float32 [3072], P('fsdp')
- grad_down_weight: float32 [3072, 768], P('fsdp')
Inputs may be any that keep to these rules, and one draw needn't show every extreme that they name: `slot_valid`: in each sequence the first 128 slots are 1; of the next 128 slots the first k are 1 and the rest 0, with k from 10 to 100, both of which occur in every draw.
All inputs are finite; a program needn't handle non-finite values.
Results may differ from a plain program's by a relative error of at most 0.02.
Values may be sent and summed in bfloat16 or wider, within the bound.
No kernel may reach another device: no remote copies, remote signals or barrier semaphores. Data moves between devices by JAX's collectives and lax.ppermute only.
A program may use at most 192 MiB of HBM per device.

v0:
```python
from functools import partial

import jax
import jax.numpy as jnp
from jax import lax
from jax.sharding import PartitionSpec as P

HEADS = 12
HD = 64


EPSILON = 1e-12
MASKED = -1e30


def normalize(values, gain, shift):
    centered = values - jnp.mean(values, axis=-1, keepdims=True)
    spread = jnp.mean(centered * centered, axis=-1, keepdims=True)
    return centered * lax.rsqrt(spread + EPSILON) * gain + shift


def column_sum(values):
    return jnp.sum(values.astype(jnp.float32), axis=0)


def body(
    layer_input,
    slot_valid,
    projections,
    out_weight,
    vectors,
    up_weight,
    up_bias,
    down_weight,
    cotangent,
):
    seq_count, slot_count, model_width = layer_input.shape
    score_scale = HD ** (-0.5)
    shape_heads = (seq_count, slot_count, HEADS, HD)
    qkv_all, out_all, vec_all = (
        lax.all_gather(projections, "fsdp", axis=1, tiled=True),
        lax.all_gather(out_weight, "fsdp", axis=0, tiled=True),
        lax.all_gather(vectors, "fsdp", axis=1, tiled=True),
    )
    in_all, bias_in_all, down_all = (
        lax.all_gather(up_weight, "fsdp", axis=0, tiled=True),
        lax.all_gather(up_bias, "fsdp", axis=0, tiled=True),
        lax.all_gather(down_weight, "fsdp", axis=0, tiled=True),
    )
    bias_q, bias_v, bias_out, gain_one, shift_one, bias_down, gain_two, shift_two = vec_all.astype(
        jnp.float32
    )
    token_rows = layer_input.reshape(-1, model_width)
    query_low = (
        jnp.dot(token_rows, qkv_all[0], preferred_element_type=jnp.float32) + bias_q
    ).astype(jnp.bfloat16)
    key_low = jnp.dot(token_rows, qkv_all[1], preferred_element_type=jnp.float32).astype(
        jnp.bfloat16
    )
    value_low = (
        jnp.dot(token_rows, qkv_all[2], preferred_element_type=jnp.float32) + bias_v
    ).astype(jnp.bfloat16)
    query_heads = query_low.reshape(shape_heads)
    key_heads = key_low.reshape(shape_heads)
    value_heads = value_low.reshape(shape_heads)
    key_live = (slot_valid > 0)[:, None, None, :]

    def scores_of():
        raw = (
            jnp.einsum(
                "nqhe,nkhe->nhqk", query_heads, key_heads, preferred_element_type=jnp.float32
            )
            * score_scale
        )
        return jnp.where(key_live, raw, MASKED)

    scores = scores_of()
    row_max = jnp.max(scores, axis=-1, keepdims=True)
    exp_scores = jnp.exp(scores - row_max)
    exp_total = jnp.sum(exp_scores, axis=-1, keepdims=True)
    log_total = row_max + jnp.log(exp_total)
    probs_low = (exp_scores / exp_total).astype(jnp.bfloat16)
    context = jnp.einsum(
        "nhqk,nkhe->nqhe", probs_low, value_heads, preferred_element_type=jnp.float32
    )
    context = context.reshape(-1, model_width).astype(jnp.bfloat16)
    first_sum = (
        token_rows.astype(jnp.float32)
        + jnp.dot(context, out_all, preferred_element_type=jnp.float32)
        + bias_out
    )
    normed, norm_one_back = jax.vjp(normalize, first_sum, gain_one, shift_one)
    normed_low = normed.astype(jnp.bfloat16)
    hidden_pre = jnp.dot(
        normed_low, in_all, preferred_element_type=jnp.float32
    ) + bias_in_all.astype(jnp.float32)
    activated, gelu_back = jax.vjp(partial(jax.nn.gelu, approximate=False), hidden_pre)
    active_low = activated.astype(jnp.bfloat16)
    second_sum = (
        normed + jnp.dot(active_low, down_all, preferred_element_type=jnp.float32) + bias_down
    )
    normed_two, norm_two_back = jax.vjp(normalize, second_sum, gain_two, shift_two)
    row_live = slot_valid.reshape(-1, 1).astype(jnp.float32)
    output = (normed_two * row_live).astype(jnp.bfloat16).reshape(layer_input.shape)
    grad_rows = cotangent.reshape(-1, model_width).astype(jnp.float32) * row_live
    grad_second, grad_gain_two, grad_shift_two = norm_two_back(grad_rows)
    grad_second_low = grad_second.astype(jnp.bfloat16)
    in_back, down_back = (
        lax.all_gather(up_weight, "fsdp", axis=0, tiled=True),
        lax.all_gather(down_weight, "fsdp", axis=0, tiled=True),
    )
    grad_down = jnp.dot(active_low.T, grad_second_low, preferred_element_type=jnp.float32)
    grad_bias_down = column_sum(grad_second_low)
    grad_active = jnp.dot(grad_second_low, down_back.T, preferred_element_type=jnp.float32)
    grad_hidden_low = gelu_back(grad_active)[0].astype(jnp.bfloat16)
    grad_up = jnp.dot(normed_low.T, grad_hidden_low, preferred_element_type=jnp.float32)
    grad_bias_up = column_sum(grad_hidden_low)
    grad_normed = grad_second_low.astype(jnp.float32) + jnp.dot(
        grad_hidden_low, in_back.T, preferred_element_type=jnp.float32
    )
    ffn_parts = (
        lax.psum_scatter(
            grad_up.astype(jnp.bfloat16), "fsdp", scatter_dimension=0, tiled=True
        ).astype(jnp.float32),
        lax.psum_scatter(
            grad_bias_up.astype(jnp.bfloat16), "fsdp", scatter_dimension=0, tiled=True
        ).astype(jnp.float32),
        lax.psum_scatter(
            grad_down.astype(jnp.bfloat16), "fsdp", scatter_dimension=0, tiled=True
        ).astype(jnp.float32),
    )
    ffn_parts = (
        lax.psum(ffn_parts[0].astype(jnp.bfloat16), "rep").astype(jnp.float32),
        lax.psum(ffn_parts[1].astype(jnp.bfloat16), "rep").astype(jnp.float32),
        lax.psum(ffn_parts[2].astype(jnp.bfloat16), "rep").astype(jnp.float32),
    )
    grad_first, grad_gain_one, grad_shift_one = norm_one_back(grad_normed)
    grad_first_low = grad_first.astype(jnp.bfloat16)
    qkv_back, out_back = (
        lax.all_gather(projections, "fsdp", axis=1, tiled=True),
        lax.all_gather(out_weight, "fsdp", axis=0, tiled=True),
    )
    grad_out = jnp.dot(context.T, grad_first_low, preferred_element_type=jnp.float32)
    grad_bias_out = column_sum(grad_first_low)
    grad_context = (
        jnp.dot(grad_first_low, out_back.T, preferred_element_type=jnp.float32)
        .astype(jnp.bfloat16)
        .reshape(shape_heads)
    )
    weights_soft = jnp.exp(scores_of() - log_total)
    probs_again = weights_soft.astype(jnp.bfloat16)
    grad_value = jnp.einsum(
        "nhqk,nqhe->nkhe", probs_again, grad_context, preferred_element_type=jnp.float32
    )
    grad_value = grad_value.reshape(-1, model_width).astype(jnp.bfloat16)
    grad_probs = jnp.einsum(
        "nqhe,nkhe->nhqk", grad_context, value_heads, preferred_element_type=jnp.float32
    )
    grad_scores = (
        weights_soft * (grad_probs - jnp.sum(weights_soft * grad_probs, axis=-1, keepdims=True))
    ).astype(jnp.bfloat16)
    grad_query = (
        jnp.einsum("nhqk,nkhe->nqhe", grad_scores, key_heads, preferred_element_type=jnp.float32)
        * score_scale
    )
    grad_query = grad_query.reshape(-1, model_width).astype(jnp.bfloat16)
    grad_key = (
        jnp.einsum("nhqk,nqhe->nkhe", grad_scores, query_heads, preferred_element_type=jnp.float32)
        * score_scale
    )
    grad_key = grad_key.reshape(-1, model_width).astype(jnp.bfloat16)
    grad_stack = jnp.stack(
        [
            jnp.dot(token_rows.T, grad_query, preferred_element_type=jnp.float32),
            jnp.dot(token_rows.T, grad_key, preferred_element_type=jnp.float32),
            jnp.dot(token_rows.T, grad_value, preferred_element_type=jnp.float32),
        ]
    )
    grad_vectors = jnp.stack(
        [
            column_sum(grad_query),
            column_sum(grad_value),
            grad_bias_out,
            grad_gain_one,
            grad_shift_one,
            grad_bias_down,
            grad_gain_two,
            grad_shift_two,
        ]
    )
    grad_total = grad_first_low.astype(jnp.float32)
    grad_total = grad_total + jnp.dot(grad_query, qkv_back[0].T, preferred_element_type=jnp.float32)
    grad_total = grad_total + jnp.dot(grad_key, qkv_back[1].T, preferred_element_type=jnp.float32)
    grad_total = grad_total + jnp.dot(grad_value, qkv_back[2].T, preferred_element_type=jnp.float32)
    grad_input = grad_total.astype(jnp.bfloat16).reshape(layer_input.shape)
    attn_parts = (
        lax.psum_scatter(
            grad_stack.astype(jnp.bfloat16), "fsdp", scatter_dimension=1, tiled=True
        ).astype(jnp.float32),
        lax.psum_scatter(
            grad_out.astype(jnp.bfloat16), "fsdp", scatter_dimension=0, tiled=True
        ).astype(jnp.float32),
        lax.psum_scatter(
            grad_vectors.astype(jnp.bfloat16), "fsdp", scatter_dimension=1, tiled=True
        ).astype(jnp.float32),
    )
    attn_parts = (
        lax.psum(attn_parts[0].astype(jnp.bfloat16), "rep").astype(jnp.float32),
        lax.psum(attn_parts[1].astype(jnp.bfloat16), "rep").astype(jnp.float32),
        lax.psum(attn_parts[2].astype(jnp.bfloat16), "rep").astype(jnp.float32),
    )
    return (
        output,
        grad_input,
        attn_parts[0],
        attn_parts[1],
        attn_parts[2],
        ffn_parts[0],
        ffn_parts[1],
        ffn_parts[2],
    )


def solution(mesh):
    placed = (
        P(("fsdp", "rep"), None, None),
        P(("fsdp", "rep"), None),
        P(None, "fsdp", None),
        P("fsdp", None),
        P(None, "fsdp"),
        P("fsdp", None),
        P("fsdp"),
        P("fsdp", None),
        P(("fsdp", "rep"), None, None),
    )
    return jax.shard_map(
        body,
        mesh=mesh,
        in_specs=placed,
        out_specs=(
            P(("fsdp", "rep"), None, None),
            P(("fsdp", "rep"), None, None),
            P(None, "fsdp", None),
            P("fsdp", None),
            P(None, "fsdp"),
            P("fsdp", None),
            P("fsdp"),
            P("fsdp", None),
        ),
        check_vma=False,
    )
```

profile of v0, /device:TPU:0, one launch (start us, length us, event | category | flops | bytes accessed | tf_op | source)
XLA Modules:
  0.0 753.9 jit_solution(702271938507066873)
XLA Ops:
  12.0 23.5 %all-gather = bf16[16,48,8]{1,2,0:T(8,128)(2,1)S(1)} all-gather(bf16[1,48,8]{1,2,0:T(8,128)(2,1)} %bitcast.138), channel_id=1, replica_groups=mesh['fsdp'=16,'rep'=2] {'fsdp'}, dimensions={0}, use_global_device_ids=true | all-gather | bytes 13056 | tf_op jit(solution)/shard_map/all_gather | solution.py:43
  38.5 31.3 %all-reduce = bf16[3072]{0:T(1024)(128)(2,1)S(1)} all-reduce(bf16[3072]{0:T(1024)(128)(2,1)S(1)} %dynamic-update-slice), channel_id=1, replica_groups=mesh['fsdp'=16,'rep'=2] {'fsdp'}, use_global_device_ids=true, to_apply=%add | all-reduce | flops 3072 | bytes 12288
  75.0 3.7 add_convert_fusion.4
  83.2 4.8 add_convert_fusion.5
  90.6 3.9 reshape.151
  97.6 3.8 fusion.6
  102.3 3.4 fusion.22
  108.5 4.0 fusion.56
  114.1 40.7 %all-gather.10.cloned.1.call-done = bf16[768,3072]{1,0:T(8,128)(2,1)} async-done(((bf16[48,3072]{1,0:T(8,128)(2,1)}), bf16[768,3072]{1,0:T(8,128)(2,1)}) %all-gather.10.cloned.1.call-update) | async-done | bytes 4718608 | tf_op jit(solution)/shard_map/all_gather | solution.py:46
  154.8 36.1 %multiply_convert_fusion.1 = (bf16[1024,3072]{1,0:T(8,128)(2,1)}, f32[1024,3072]{1,0:T(8,128)}, f32[1024,3072]{1,0:T(8,128)}) fusion(f32[3072]{0:T(1024)S(1)} %convert_element_type.182, bf16[768,3072]{1,0:T(8,128)(2,1)} %all-gather.10.cloned.1.call-done, f32[1024,768]{1,0:T(8,128)S(1)} %get-tuple-element.69, f32[768]{0:T(1024)S(1)} %get-tuple-element.40, ...), kind=kOutput, calls=%fused_computation.6 | convolution fusion | flops 5043388416 | bytes 39348224 | tf_op jit(solution)/shard_map/dot_general | solution.py:94
  190.9 17.7 %all-gather.12.cloned.1.call-done = bf16[3072,768]{1,0:T(8,128)(2,1)} async-done(((bf16[192,768]{1,0:T(8,128)(2,1)}), bf16[3072,768]{1,0:T(8,128)(2,1)}) %all-gather.12.cloned.1.call-update) | async-done | bytes 4718608 | tf_op jit(solution)/shard_map/all_gather | solution.py:48
  208.7 8.8 %fusion.57 = (f32[1024]{0:T(1024)S(1)}, f32[1024,768]{1,0:T(8,128)S(1)}) fusion(f32[768]{0:T(1024)S(1)} %get-tuple-element.39, bf16[1024,3072]{1,0:T(8,128)(2,1)} %get-tuple-element.59, bf16[3072,768]{1,0:T(8,128)(2,1)} %all-gather.12.cloned.1.call-done, f32[768]{0:T(1024)S(1)} %get-tuple-element.40, f32[768]{0:T(1024)S(1)} %get-tuple-element.41, ...), kind=kOutput, calls=%fused_computation.120 | convolution fusion | flops 4837342208 | bytes 17323008 | tf_op jit(solution)/shard_map/dot_general | solution.py:100
  223.7 17.3 %fusion.60 = (bf16[3072]{0:T(1024)(128)(2,1)S(1)}, bf16[1024,3072]{1,0:T(8,128)(2,1)}) fusion(f32[1024,3072]{1,0:T(8,128)} %get-tuple-element.60, bf16[1024,768]{1,0:T(8,128)(2,1)S(1)} %get-tuple-element.52, bf16[3072,768]{1,0:T(8,128)(2,1)} %all-gather.12.cloned.1.call-done, f32[1024,3072]{1,0:T(8,128)} %get-tuple-element.70, ...), kind=kOutput, calls=%fused_computation.123 | convolution fusion | flops 4882166784 | bytes 37767168 | tf_op jit(solution)/shard_map/dot_general | solution.py:114
  241.0 9.7 %multiply_reduce_fusion.3 = (bf16[768]{0:T(1024)(128)(2,1)S(1)}, f32[1024]{0:T(1024)S(1)}, bf16[768]{0:T(1024)(128)(2,1)S(1)}, f32[1024,768]{1,0:T(8,128)S(1)}) fusion(f32[1024,768]{1,0:T(8,128)S(1)} %copy-done.7, f32[1024]{0:T(1024)S(1)} %fusion.40, f32[1024]{0:T(1024)S(1)} %broadcast_multiply_fusion.1, f32[768]{0:T(1024)S(1)} %get-tuple-element.41, ...), kind=kOutput, calls=%fused_computation.37 | convolution fusion | flops 4839699456 | bytes 18892800 | tf_op jit(solution)/shard_map/dot_general | solution.py:118
  258.9 3.9 reshape.155
  262.8 8.6 %multiply_reduce_fusion = (f32[4,12,256]{2,1,0:T(8,128)S(1)}, f32[4,12,256,256]{2,3,1,0:T(8,128)S(1)}) fusion(f32[4,12,256]{2,1,0:T(8,128)S(1)} %copy-done.20, f32[4,12,256,256]{2,3,1,0:T(8,128)} %copy-done, pred[4,256]{1,0:T(4,128)(4,1)S(1)} %copy-done.22, bf16[4,256,12,64]{1,0,3,2:T(4,128)(2,1)S(1)} %copy-done.9, bf16[4,256,12,64]{1,0,3,2:T(4,128)(2,1)} %reshape.155), kind=kOutput, calls=%fused_computation.3 | convolution fusion | flops 418369536 | bytes 28410880 | tf_op jit(solution)/shard_map/nqhe,nkhe->nhqk/dot_general | solution.py:156
  271.4 8.0 %multiply_convert_fusion = bf16[4,12,256,256]{2,3,1,0:T(8,128)(2,1)S(1)} fusion(f32[4,12,256,256]{2,3,1,0:T(8,128)S(1)} %get-tuple-element.75, f32[4,12,256]{2,1,0:T(8,128)S(1)} %get-tuple-element.74, f32[4,12,256]{2,1,0:T(8,128)S(1)} %copy-done.20, f32[4,12,256,256]{2,3,1,0:T(8,128)} %copy-done, pred[4,256]{1,0:T(4,128)(4,1)S(1)} %copy-done.22), kind=kLoop, calls=%fused_computation.2 | loop fusion | flops 18874368 | bytes 31556608 | tf_op jit(solution)/shard_map/convert_element_type | solution.py:161
  285.2 3.6 fusion.59
  300.3 8.1 %copy.73 = bf16[3,768,768]{2,0,1:T(4,128)(2,1)} copy(bf16[3,768,768]{1,2,0:T(8,128)(2,1)} %pad_maximum_fusion) | data formatting | bytes 7077888 | tf_op jit(solution)/shard_map/stack | solution.py:172
  309.9 3.8 convolution_convert_fusion.4
  313.7 10.7 %convolution_convert_fusion.1 = bf16[768,3072]{1,0:T(8,128)(2,1)} fusion(bf16[1024,3072]{1,0:T(8,128)(2,1)} %get-tuple-element.81, f32[1024,768]{1,0:T(8,128)} %copy-done.6, f32[768]{0:T(1024)S(1)} %get-tuple-element.40, f32[768]{0:T(1024)S(1)} %get-tuple-element.41, f32[1024]{0:T(1024)S(1)} %fusion.40, f32[1024]{0:T(1024)S(1)} %broadcast_multiply_fusion.1), kind=kOutput, calls=%fused_computation.30 | convolution fusion | flops 4838129664 | bytes 14170112 | tf_op jit(solution)/shard_map/dot_general | solution.py:116
  324.5 9.3 %convolution_convert_fusion = bf16[3072,768]{1,0:T(8,128)(2,1)} fusion(bf16[1024,3072]{1,0:T(8,128)(2,1)} %get-tuple-element.59, bf16[1024,768]{1,0:T(8,128)(2,1)} %copy-done.16), kind=kOutput, calls=%fused_computation.29 | convolution fusion | flops 4834197504 | bytes 12582912 | tf_op jit(solution)/shard_map/dot_general | solution.py:112
  337.2 32.7 %all-reduce.2 = bf16[3072]{0:T(1024)(128)(2,1)S(1)} all-reduce(bf16[3072]{0:T(1024)(128)(2,1)S(1)} %get-tuple-element.80), channel_id=6, replica_groups=mesh['fsdp'=16,'rep'=2] {'fsdp'}, use_global_device_ids=true, to_apply=%region_28.29.clone | all-reduce | flops 3072 | bytes 12288
  370.1 5.1 fusion.39
  375.1 49.2 %all-reduce.8.cloned.1.call-done = bf16[3,768,768]{2,0,1:T(4,128)(2,1)} async-done(((bf16[3,768,768]{2,0,1:T(4,128)(2,1)}), bf16[3,768,768]{2,0,1:T(4,128)(2,1)}) %all-reduce.8.cloned.1.call-update) | async-done | bytes 3538960
  426.1 59.6 %reduce-scatter.7.cloned.1.call-done = bf16[48,768]{1,0:T(8,128)(2,1)} async-done(((bf16[768,768]{1,0:T(8,128)(2,1)}), bf16[48,768]{1,0:T(8,128)(2,1)}) %reduce-scatter.7.cloned.1.call-update) | async-done | bytes 73744 | tf_op jit(solution)/shard_map/reduce_scatter | solution.py:200
  485.7 78.6 %reduce-scatter.9.cloned.1.call-done = bf16[48,3072]{1,0:T(8,128)(2,1)} async-done(((bf16[768,3072]{1,0:T(8,128)(2,1)}), bf16[48,3072]{1,0:T(8,128)(2,1)}) %reduce-scatter.9.cloned.1.call-update) | async-done | bytes 294928 | tf_op jit(solution)/shard_map/reduce_scatter | solution.py:122
  564.3 78.7 %reduce-scatter.11.cloned.1.call-done = bf16[192,768]{1,0:T(8,128)(2,1)} async-done(((bf16[3072,768]{1,0:T(8,128)(2,1)}), bf16[192,768]{1,0:T(8,128)(2,1)}) %reduce-scatter.11.cloned.1.call-update) | async-done | bytes 294928 | tf_op jit(solution)/shard_map/reduce_scatter | solution.py:128
  645.9 3.9 add_convert_fusion.1
  649.8 49.6 %reduce-scatter.13.cloned.1.call-done = bf16[48,8]{1,0:T(8,128)(2,1)} async-done(((bf16[768,8]{1,0:T(8,128)(2,1)}), bf16[48,8]{1,0:T(8,128)(2,1)}) %reduce-scatter.13.cloned.1.call-update) | async-done | bytes 784
  700.3 4.9 all-reduce.3
  706.3 33.3 %all-reduce.10.cloned.1.call-done = (bf16[3,48,768]{2,0,1:T(4,128)(2,1)}, bf16[48,768]{1,0:T(8,128)(2,1)}, bf16[48,3072]{1,0:T(8,128)(2,1)}, bf16[192,768]{1,0:T(8,128)(2,1)}) async-done(((bf16[3,48,768]{2,0,1:T(4,128)(2,1)}, bf16[48,768]{1,0:T(8,128)(2,1)}, bf16[48,3072]{1,0:T(8,128)(2,1)}, bf16[192,768]{1,0:T(8,128)(2,1)}), (bf16[3,48,768]{2,0,1:T(4,128)(2,1)}, bf16[48,768]{1,0:T(8,128)(2,1)}, ...) | async-done | bytes 884752 | tf_op jit(solution)/shard_map/psum | solution.py:208
  (151 shorter events, 76.3 us)
Async XLA Ops:
  7.2 62.7 %all-gather.6.cloned.1.call-start = ((), (), s32[]{:S(2)}) async-start(), calls=%async_computation.4 | async-start | bytes 3760128 | tf_op jit(solution)/shard_map/all_gather | solution.py:41
  7.9 100.6 %all-gather.8.cloned.1.call-start = ((), (), s32[]{:S(2)}) async-start(), calls=%async_computation.5 | async-start | bytes 1253376 | tf_op jit(solution)/shard_map/all_gather | solution.py:42
  8.6 146.2 %all-gather.10.cloned.1.call-start = ((), (), s32[]{:S(2)}) async-start(), calls=%async_computation.6 | async-start | bytes 5013504 | tf_op jit(solution)/shard_map/all_gather | solution.py:46
  9.4 199.3 %all-gather.12.cloned.1.call-start = ((), (), s32[]{:S(2)}) async-start(), calls=%async_computation.7 | async-start | bytes 5013504 | tf_op jit(solution)/shard_map/all_gather | solution.py:48
  10.0 414.4 %all-reduce.8.cloned.1.call-start = ((), (), s32[]{:S(2)}) async-start(), calls=%async_computation.12 | async-start | bytes 9437184
  10.7 90.7 %copy-start.21 = (pred[4,256]{1,0:T(4,128)(4,1)}, pred[4,256]{1,0:T(4,128)(4,1)S(1)}, u32[]{:S(2)}) copy-start(pred[4,256]{1,0:T(4,128)(4,1)S(1)} %broadcast_compare_fusion) | copy-start | bytes 3076
  75.0 19.5 %copy-start.4 = (bf16[4,256,12,64]{1,0,3,2:T(4,128)(2,1)}, bf16[4,256,12,64]{1,0,3,2:T(4,128)(2,1)S(1)}, u32[]{:S(2)}) copy-start(bf16[4,256,12,64]{1,0,3,2:T(4,128)(2,1)S(1)} %reshape.153) | copy-start | bytes 4718596
  83.2 11.3 %copy-start.1 = (bf16[4,256,12,64]{1,0,3,2:T(4,128)(2,1)}, bf16[4,256,12,64]{1,0,3,2:T(4,128)(2,1)S(1)}, u32[]{:S(2)}) copy-start(bf16[4,256,12,64]{1,0,3,2:T(4,128)(2,1)S(1)} %reshape.152) | copy-start | bytes 4718596
  97.6 4.8 copy-start
  97.6 4.7 copy-start.8
  112.5 96.1 %copy-start.6 = (f32[1024,768]{1,0:T(8,128)}, f32[1024,768]{1,0:T(8,128)S(1)}, u32[]{:S(2)}) copy-start(f32[1024,768]{1,0:T(8,128)S(1)} %get-tuple-element.69) | copy-start | bytes 9437188
  223.6 17.3 %copy-start.16 = (bf16[1024,768]{1,0:T(8,128)(2,1)}, bf16[1024,768]{1,0:T(8,128)(2,1)S(1)}, u32[]{:S(2)}) copy-start(bf16[1024,768]{1,0:T(8,128)(2,1)S(1)} %get-tuple-element.52) | copy-start | bytes 4718596
  223.6 17.3 %copy-start.7 = (f32[1024,768]{1,0:T(8,128)S(1)}, f32[1024,768]{1,0:T(8,128)}, u32[]{:S(2)}) copy-start(f32[1024,768]{1,0:T(8,128)} %copy-done.6) | copy-start | bytes 9437188
  256.2 6.6 copy-start.9
  256.2 6.6 copy-start.20
  256.2 6.6 copy-start.22
  271.4 8.1 %copy-start.2 = (bf16[4,256,12,64]{1,0,3,2:T(4,128)(2,1)S(1)}, bf16[4,256,12,64]{1,0,3,2:T(4,128)(2,1)}, u32[]{:S(2)}) copy-start(bf16[4,256,12,64]{1,0,3,2:T(4,128)(2,1)} %copy-done.1) | copy-start | bytes 4718596
  279.5 2.0 copy-start.5
  279.5 3.4 slice-start
  279.5 3.9 slice-start.1
  281.5 3.3 slice-start.2
  281.5 3.7 copy-start.10
  290.4 5.0 copy-start.19
  292.0 4.8 copy-start.17
  308.5 177.2 %reduce-scatter.7.cloned.1.call-start = ((), (), s32[]{:S(2)}) async-start(), calls=%async_computation.8 | async-start | bytes 1253376 | tf_op jit(solution)/shard_map/reduce_scatter | solution.py:200
  313.7 250.6 %reduce-scatter.9.cloned.1.call-start = ((), (), s32[]{:S(2)}) async-start(), calls=%async_computation.9 | async-start | bytes 5013504 | tf_op jit(solution)/shard_map/reduce_scatter | solution.py:122
  324.4 318.5 %reduce-scatter.11.cloned.1.call-start = ((), (), s32[]{:S(2)}) async-start(), calls=%async_computation.10 | async-start | bytes 5013504 | tf_op jit(solution)/shard_map/reduce_scatter | solution.py:128
  333.8 365.7 %reduce-scatter.13.cloned.1.call-start = ((), (), s32[]{:S(2)}) async-start(), calls=%async_computation.11 | async-start | bytes 208896
  369.9 369.7 %all-reduce.10.cloned.1.call-start = ((), (), s32[]{:S(2)}) async-start(), calls=%async_computation.13 | async-start | bytes 1916928 | tf_op jit(solution)/shard_map/psum | solution.py:208
  370.1 272.9 %copy-start.18 = (bf16[96,8,4,256]{3,1,2,0:T(8,128)(2,1)S(1)}, bf16[96,8,4,256]{3,1,2,0:T(8,128)(2,1)}, u32[]{:S(2)}) copy-start(bf16[96,8,4,256]{3,1,2,0:T(8,128)(2,1)} %copy-done.17) | copy-start | bytes 4718596
  643.0 2.9 copy-start.14
  643.0 2.9 copy-start.15
  (7 other events, 9.9 us)
Sparse Core Ops, SparseCore 0:
  10.3 50.7 all-gather.5
  63.3 37.0 all-gather.7
  102.8 51.9 all-gather.9
  156.9 51.6 all-gather.11
  308.6 115.6 all-reduce.7
  427.8 57.8 reduce-scatter.6
  489.6 74.6 reduce-scatter.8
  568.2 74.7 reduce-scatter.10
  647.0 52.4 reduce-scatter.12
  702.4 37.1 all-reduce.9
where the time goes:
time: 765 us; the launch traced here: 754 us
  waiting for transfers between devices  410 us (54%)
  matrix products  152 us (20%)
  blocking collectives  92.3 us (12%)
  local copies, waits for them, and re-layouts  50.5 us (7%)
  other arithmetic  31.3 us (4%)
  between operations  17.2 us (2%)
    unnamed x12, waiting for transfers between devices  102 us
    reduce_scatter x1, waiting for transfers between devices, body(): lax.psum_scatter(grad_down.astype(jnp.bfloat16), 'fsdp', scatter_dimensio...  78.7 us
    reduce_scatter x1, waiting for transfers between devices, body(): lax.psum_scatter(grad_up.astype(jnp.bfloat16), 'fsdp', scatter_dimension=...  78.6 us
    unnamed x2, blocking collectives  64 us
    reduce_scatter x1, waiting for transfers between devices, body(): lax.psum_scatter(grad_out.astype(jnp.bfloat16), 'fsdp', scatter_dimension...  59.6 us
    all_gather x1, waiting for transfers between devices, body(): lax.all_gather(up_weight, 'fsdp', axis=0, tiled=True)  40.7 us
    dot_general x1, matrix products, body(): jnp.dot(normed_low, in_all, preferred_element_type=jnp.float32)  36.1 us
    psum x1, waiting for transfers between devices, body(): lax.psum(attn_parts[0].astype(jnp.bfloat16), 'rep').astype(jnp.float32)  33.3 us
  transfers between devices with their start and end apart: 10, of which 8 were waited for; matrix products, arithmetic and copies ran while one was open for 17% of the time, Pallas kernels for 0%

commit v1 on v0

v1 whole, which is shorter than its diff:
```python
from functools import partial

import jax
import jax.numpy as jnp
from jax import lax
from jax.experimental import pallas as pl
from jax.experimental.pallas import tpu as pltpu
from jax.sharding import PartitionSpec as P

HEADS = 12
HD = 64
PAIR = 2 * HD
SMALL_ROWS = 8
EPSILON = 1e-12
MASKED = -1e30
F32 = jnp.float32
BF16 = jnp.bfloat16
NN = (((1,), (0,)), ((), ()))
NT = (((1,), (1,)), ((), ()))
TN = (((0,), (0,)), ((), ()))


def mm(lhs, rhs, dims=NN):
    return lax.dot_general(lhs, rhs, dims, preferred_element_type=F32)


def square(ref, start, count):
    taken = ref[:, start : start + count, :]
    return taken.reshape(-1, taken.shape[-1])


def lane_masks(scale):
    lane = lax.broadcasted_iota(jnp.int32, (1, PAIR), 1)
    even = jnp.where(lane < HD, scale, 0.0).astype(BF16)
    odd = jnp.where(lane < HD, 0.0, scale).astype(BF16)
    return even, odd


def split_heads(pair, scale):
    even, odd = lane_masks(scale)
    return jnp.concatenate([pair * even, pair * odd], axis=0)


def join_heads(stacked):
    half = stacked.shape[0] // 2
    lane = lax.broadcasted_iota(jnp.int32, (half, PAIR), 1)
    return jnp.where(lane < HD, stacked[:half], stacked[half:])


def column_sum(values):
    return jnp.sum(values.astype(F32), axis=0, keepdims=True)


def attend_kernel(rows, x_ref, live_ref, w_ref, vec_ref, q_ref, k_ref, v_ref, p_ref, c_ref, f_ref):
    x = x_ref[0]
    q_ref[0] = (mm(x, square(w_ref, 0, rows)) + vec_ref[0:1]).astype(BF16)
    k_ref[0] = mm(x, square(w_ref, rows, rows)).astype(BF16)
    v_ref[0] = (mm(x, square(w_ref, 2 * rows, rows)) + vec_ref[1:2]).astype(BF16)
    live = live_ref[0] > 0.0
    for pair in range(HEADS // 2):
        cols = slice(pair * PAIR, (pair + 1) * PAIR)
        stacked = split_heads(q_ref[0, :, cols], HD**-0.5)
        scores = jnp.where(live, mm(k_ref[0, :, cols], stacked, NT), MASKED)
        raised = jnp.exp(scores - jnp.max(scores, axis=0, keepdims=True))
        weights = raised * (1.0 / jnp.sum(raised, axis=0, keepdims=True))
        p_ref[0, pair] = weights
        context = mm(weights.astype(BF16), v_ref[0, :, cols], TN)
        c_ref[0, :, cols] = join_heads(context).astype(BF16)
    f_ref[0] = x.astype(F32) + mm(c_ref[0], square(w_ref, 3 * rows, rows)) + vec_ref[2:3]


def centre(values):
    centered = values - jnp.mean(values, axis=-1, keepdims=True)
    spread = jnp.mean(centered * centered, axis=-1, keepdims=True)
    rate = lax.rsqrt(spread + EPSILON)
    return centered * rate, rate


def centre_back(grad, unit, rate):
    return rate * (
        grad
        - jnp.mean(grad, axis=-1, keepdims=True)
        - unit * jnp.mean(grad * unit, axis=-1, keepdims=True)
    )


def accumulate(ref, first, value):
    @pl.when(first)
    def _():
        ref[...] = value

    @pl.when(jnp.logical_not(first))
    def _():
        ref[...] += value


def feed_kernel(
    rows,
    hidden,
    f_ref,
    live_ref,
    cot_ref,
    w_ref,
    vec_ref,
    bias_ref,
    o_ref,
    act_ref,
    gh_ref,
    gs_ref,
    gf_ref,
    n_ref,
    small_ref,
    gbias_ref,
    slope_ref,
):
    width = f_ref.shape[-1]
    folds = act_ref.shape[-1] // width
    shards = max(width // hidden, 1)

    def up(fold):
        return square(w_ref, fold * rows, rows)

    def down(fold):
        base = folds * rows
        if hidden >= width:
            return square(w_ref, base + fold * width, width)
        taken = w_ref[fold * shards : (fold + 1) * shards, base : base + hidden, :]
        return taken.reshape(width, width)

    gain_one, shift_one, gain_two, shift_two = (vec_ref[i : i + 1] for i in (3, 4, 6, 7))
    unit_one, rate_one = centre(f_ref[...])
    normed = unit_one * gain_one + shift_one
    n_ref[...] = normed.astype(BF16)
    second = normed + vec_ref[5:6]
    for fold in range(folds):
        cols = slice(fold * width, (fold + 1) * width)
        pre = mm(n_ref[...], up(fold)) + bias_ref[:, cols]
        phi = 0.5 + 0.5 * lax.erf(pre * 0.7071067811865476)
        act = (pre * phi).astype(BF16)
        act_ref[:, cols] = act
        slope_ref[:, cols] = phi + pre * (jnp.exp(pre * pre * -0.5) * 0.3989422804014327)
        second = second + mm(act, down(fold))
    unit_two, rate_two = centre(second)
    live = live_ref[...]
    o_ref[...] = ((unit_two * gain_two + shift_two) * live).astype(BF16)
    grad_rows = cot_ref[...].astype(F32) * live
    grad_second = centre_back(grad_rows * gain_two, unit_two, rate_two).astype(BF16)
    gs_ref[...] = grad_second
    grad_normed = grad_second.astype(F32)
    grad_bias = []
    for fold in range(folds):
        cols = slice(fold * width, (fold + 1) * width)
        grad_hidden = (mm(gs_ref[...], down(fold), NT) * slope_ref[:, cols]).astype(BF16)
        gh_ref[:, cols] = grad_hidden
        grad_bias.append(column_sum(grad_hidden))
        grad_normed = grad_normed + mm(grad_hidden, up(fold), NT)
    grad_first = centre_back(grad_normed * gain_one, unit_one, rate_one).astype(BF16)
    gf_ref[...] = grad_first
    first = pl.program_id(0) == 0
    blank = jnp.zeros((2, width), F32)
    small = [
        column_sum(grad_first),
        column_sum(grad_normed * unit_one),
        column_sum(grad_normed),
        column_sum(grad_second),
        column_sum(grad_rows * unit_two),
        column_sum(grad_rows),
        blank,
    ]
    accumulate(small_ref, first, jnp.concatenate(small, axis=0))
    accumulate(gbias_ref, first, jnp.concatenate(grad_bias, axis=1))


def attend_back_kernel(rows, g_ref, w_ref, q_ref, k_ref, v_ref, p_ref, d_ref, gi_ref, small_ref):
    width = g_ref.shape[-1]
    grad_context = mm(g_ref[0], square(w_ref, 3 * rows, rows), NT).astype(BF16)
    for pair in range(HEADS // 2):
        cols = slice(pair * PAIR, (pair + 1) * PAIR)
        stacked = split_heads(grad_context[:, cols], 1.0)
        weights = p_ref[0, pair]
        grad_value = mm(weights.astype(BF16), stacked)
        grad_probs = mm(v_ref[0, :, cols], stacked, NT)
        inner = jnp.sum(weights * grad_probs, axis=0, keepdims=True)
        grad_scores = (weights * (grad_probs - inner)).astype(BF16)
        grad_key = mm(grad_scores, split_heads(q_ref[0, :, cols], HD**-0.5))
        grad_query = join_heads(mm(grad_scores, k_ref[0, :, cols], TN)) * HD**-0.5
        for part, grad in enumerate((grad_query, grad_key, grad_value)):
            at = part * width + pair * PAIR
            d_ref[0, :, at : at + PAIR] = grad.astype(BF16)
    total = g_ref[0].astype(F32)
    for part in range(3):
        grad = d_ref[0, :, part * width : (part + 1) * width]
        total = total + mm(grad, square(w_ref, part * rows, rows), NT)
    gi_ref[0] = total.astype(BF16)
    small = [
        column_sum(d_ref[0, :, :width]),
        column_sum(d_ref[0, :, 2 * width :]),
        jnp.zeros((6, width), F32),
    ]
    accumulate(small_ref, pl.program_id(0) == 0, jnp.concatenate(small, axis=0))


def whole(array):
    return pl.BlockSpec(
        array.shape, lambda i: (0,) * array.ndim, pipeline_mode=pl.Buffered(1)
    )


def kept(shape):
    return pl.BlockSpec(shape, lambda i: (0,) * len(shape))


def per_step(shape):
    return pl.BlockSpec((1,) + shape[1:], lambda i: (i,) + (0,) * (len(shape) - 1))


def shaped(shape, dtype):
    return jax.ShapeDtypeStruct(shape, dtype)


def attend(tokens, live, weights, rows, vec):
    seqs, slots, width = tokens.shape
    low = shaped((seqs, slots, width), BF16)
    outs = (
        low,
        low,
        low,
        shaped((seqs, HEADS // 2, slots, 2 * slots), F32),
        low,
        shaped((seqs, slots, width), F32),
    )
    return pl.pallas_call(
        partial(attend_kernel, rows),
        grid=(seqs,),
        in_specs=[per_step(tokens.shape), per_step(live.shape), whole(weights), whole(vec)],
        out_specs=tuple(per_step(out.shape) for out in outs),
        out_shape=outs,
        name="attend",
    )(tokens, live, weights, vec)


def feed(first_sum, live, cotangent, weights, rows, hidden, vec, bias):
    count, width = first_sum.shape
    block = 512 if count % 512 == 0 else 256
    inner = bias.shape[1]

    def tall(columns):
        return pl.BlockSpec((block, columns), lambda i: (i, 0))

    low = shaped((count, width), BF16)
    wide = shaped((count, inner), BF16)
    return pl.pallas_call(
        partial(feed_kernel, rows, hidden),
        grid=(count // block,),
        in_specs=[tall(width), tall(1), tall(width), whole(weights), whole(vec), whole(bias)],
        out_specs=(
            tall(width),
            tall(inner),
            tall(inner),
            tall(width),
            tall(width),
            tall(width),
            kept((8, width)),
            kept((1, inner)),
        ),
        out_shape=(low, wide, wide, low, low, low, shaped((8, width), F32), shaped((1, inner), F32)),
        scratch_shapes=[pltpu.VMEM((block, inner), F32)],
        name="feed",
    )(first_sum, live, cotangent, weights, vec, bias)


def attend_back(grad_first, weights, rows, query, key, value, probs):
    seqs, slots, width = grad_first.shape
    outs = (
        shaped((seqs, slots, 3 * width), BF16),
        shaped((seqs, slots, width), BF16),
        shaped((8, width), F32),
    )
    return pl.pallas_call(
        partial(attend_back_kernel, rows),
        grid=(seqs,),
        in_specs=[
            per_step(grad_first.shape),
            whole(weights),
            per_step(query.shape),
            per_step(query.shape),
            per_step(query.shape),
            per_step(probs.shape),
        ],
        out_specs=(per_step(outs[0].shape), per_step(outs[1].shape), kept((8, width))),
        out_shape=outs,
        name="attend_back",
    )(grad_first, weights, query, key, value, probs)


def scattered(packed):
    own = lax.psum_scatter(packed, "fsdp", scatter_dimension=0, tiled=True)[0]
    if lax.axis_size("rep") == 2:
        other = lax.ppermute(own, "rep", [(0, 1), (1, 0)])
        return own.astype(F32) + other.astype(F32)
    return lax.psum(own, "rep").astype(F32)


def unsharded(packed, sizes):
    pieces, at = [], 0
    for size in sizes:
        pieces.append(packed[:, at : at + size].reshape(-1, packed.shape[-1]))
        at += size
    return jnp.concatenate(pieces)[None]


def body(
    layer_input,
    slot_valid,
    projections,
    out_weight,
    vectors,
    up_weight,
    up_bias,
    down_weight,
    cotangent,
):
    seq_count, slot_count, width = layer_input.shape
    fsdp_size = lax.axis_size("fsdp")
    own_rows = out_weight.shape[0]
    hidden_own = down_weight.shape[0]
    folds = up_weight.shape[1] // width
    small = jnp.concatenate([vectors.reshape(-1), up_bias])
    small = jnp.pad(small, (0, SMALL_ROWS * width - small.size)).reshape(SMALL_ROWS, -1)
    attn_own = jnp.concatenate([projections.reshape(-1, width), out_weight, small])
    attn_all = lax.all_gather(attn_own, "fsdp", axis=0)
    ffn_own = jnp.concatenate(
        [up_weight[:, i * width : (i + 1) * width] for i in range(folds)] + [down_weight]
    )
    ffn_own = lax.optimization_barrier((ffn_own, attn_own))[0]
    ffn_all = lax.all_gather(ffn_own, "fsdp", axis=0)
    small_all = attn_all[:, 4 * own_rows :].reshape(fsdp_size, -1)
    vec_count = vectors.shape[0] * own_rows
    vec_all = (
        small_all[:, :vec_count]
        .reshape(fsdp_size, -1, own_rows)
        .transpose(1, 0, 2)
        .reshape(-1, width)
        .astype(F32)
    )
    bias_all = small_all[:, vec_count : vec_count + hidden_own].reshape(1, -1).astype(F32)
    attn_rows, ffn_rows, ffn_hidden = own_rows, own_rows, hidden_own
    if own_rows % 16:
        attn_all = unsharded(attn_all, [own_rows] * 4)
        ffn_all = unsharded(ffn_all, [own_rows] * folds + [hidden_own])
        attn_rows, ffn_rows, ffn_hidden = width, width, folds * width
    live = slot_valid.astype(F32)[:, :, None]
    query, key, value, probs, context, first_sum = attend(
        layer_input, live, attn_all, attn_rows, vec_all
    )
    token_count = seq_count * slot_count
    output, active, grad_hidden, grad_second, grad_first, normed, ffn_small, grad_bias = feed(
        first_sum.reshape(token_count, width),
        live.reshape(token_count, 1),
        cotangent.reshape(token_count, width),
        ffn_all,
        ffn_rows,
        ffn_hidden,
        vec_all,
        bias_all,
    )
    grad_down = jnp.dot(active.T, grad_second, preferred_element_type=F32).astype(BF16)
    grad_up = jnp.dot(normed.T, grad_hidden, preferred_element_type=F32).astype(BF16)
    up_blocks = grad_up.reshape(fsdp_size, own_rows, folds, width)
    ffn_parts = scattered(
        jnp.concatenate(
            [up_blocks[:, :, i] for i in range(folds)]
            + [grad_down.reshape(fsdp_size, hidden_own, width)],
            axis=1,
        )
    )
    grad_qkv, grad_input, attn_small = attend_back(
        grad_first.reshape(seq_count, slot_count, width), attn_all, attn_rows, query, key, value, probs
    )
    grad_out = jnp.dot(
        context.reshape(token_count, width).T, grad_first, preferred_element_type=F32
    )
    grad_stack = jnp.dot(
        layer_input.reshape(token_count, width).T,
        grad_qkv.reshape(token_count, 3 * width),
        preferred_element_type=F32,
    ).astype(BF16)
    grad_vectors = jnp.concatenate([attn_small[:2], ffn_small[:6]])
    small_grad = jnp.concatenate(
        [
            grad_vectors.reshape(-1, fsdp_size, own_rows).transpose(1, 0, 2).reshape(fsdp_size, -1),
            grad_bias.reshape(fsdp_size, -1),
        ],
        axis=1,
    ).astype(BF16)
    small_grad = jnp.pad(
        small_grad, ((0, 0), (0, SMALL_ROWS * width - small_grad.shape[1]))
    ).reshape(fsdp_size, SMALL_ROWS, width)
    attn_parts = scattered(
        jnp.concatenate(
            [
                grad_stack[:, i * width : (i + 1) * width].reshape(fsdp_size, own_rows, width)
                for i in range(3)
            ]
            + [grad_out.astype(BF16).reshape(fsdp_size, own_rows, width), small_grad],
            axis=1,
        )
    )
    small_part = attn_parts[4 * own_rows :].reshape(-1)
    return (
        output.reshape(layer_input.shape),
        grad_input,
        attn_parts[: 3 * own_rows].reshape(3, own_rows, width),
        attn_parts[3 * own_rows : 4 * own_rows],
        small_part[:vec_count].reshape(-1, own_rows),
        jnp.concatenate(
            [ffn_parts[i * own_rows : (i + 1) * own_rows] for i in range(folds)], axis=1
        ),
        small_part[vec_count : vec_count + hidden_own],
        ffn_parts[folds * own_rows :],
    )


def solution(mesh):
    rows3 = P(("fsdp", "rep"), None, None)
    third = P(None, "fsdp", None)
    tall = P("fsdp", None)
    return jax.shard_map(
        body,
        mesh=mesh,
        in_specs=(
            rows3,
            P(("fsdp", "rep"), None),
            third,
            tall,
            P(None, "fsdp"),
            tall,
            P("fsdp"),
            tall,
            rows3,
        ),
        out_specs=(rows3, rows3, third, tall, P(None, "fsdp"), tall, P("fsdp"), tall),
        check_vma=False,
    )
```

time: 765 us -> 441 us (0.58); the launches traced: 754 us -> 440 us
  waiting for transfers between devices: 410 us -> 268 us
  matrix products: 152 us -> 22.6 us
  blocking collectives: 92.3 us -> 0 us
  Pallas kernels: 0 us -> 75.5 us
  other arithmetic: 31.3 us -> 4.46 us
    dot_general x24 -> x4, matrix products: 152 us -> 22.6 us  [the longest x1 9.15 us: body(): jnp.dot(normed.T, grad_hidden, preferred_element_type=F32).astype(BF16)]
    unnamed x12 -> x4, waiting for transfers between devices: 102 us -> 0.07 us
    pallas_call x0 -> x3, Pallas kernels: none -> 75.5 us  [the longest x1 35.1 us: feed(): pl.pallas_call(partial(feed_kernel, rows, hidden), grid=(count // block,)...]
    reduce_scatter x3 -> x2, waiting for transfers between devices: 217 us -> 149 us  [scattered(): own = lax.psum_scatter(packed, 'fsdp', scatter_dimension=0, tiled=True)[0]]
    unnamed x2 -> x0, blocking collectives: 64 us -> none
    all_gather x4 -> x2, waiting for transfers between devices: 58.4 us -> 113 us  [the longest x1 63.4 us: body(): ffn_all = lax.all_gather(ffn_own, 'fsdp', axis=0)]
    psum x1 -> x0, waiting for transfers between devices: 33.3 us -> none  [body(): lax.psum(attn_parts[0].astype(jnp.bfloat16), 'rep').astype(jnp.float32)]
    all_gather x1 -> x0, blocking collectives: 23.5 us -> none  [body(): lax.all_gather(vectors, 'fsdp', axis=1, tiled=True)]
  transfers between devices with their start and end apart: 10 -> 6, of which waited for: 8 -> 5; matrix products, arithmetic and copies ran while one was open for 17% -> 6% of each run, Pallas kernels for 0% -> 9%
where the time goes in v1:
time: 441 us; the launch traced here: 440 us
  waiting for transfers between devices  268 us (61%)
  Pallas kernels  75.5 us (17%)
  local copies, waits for them, and re-layouts  52.6 us (12%)
  matrix products  22.6 us (5%)
  between operations  14 us (3%)
  other arithmetic  4.46 us (1%)
    reduce_scatter x2, waiting for transfers between devices, scattered(): own = lax.psum_scatter(packed, 'fsdp', scatter_dimension=0, tiled=True)[0]  149 us
    all_gather x1, waiting for transfers between devices, body(): ffn_all = lax.all_gather(ffn_own, 'fsdp', axis=0)  63.4 us
    all_gather x1, waiting for transfers between devices, body(): attn_all = lax.all_gather(attn_own, 'fsdp', axis=0)  49.6 us
    pallas_call x1, Pallas kernels, feed(): pl.pallas_call(partial(feed_kernel, rows, hidden), grid=(count // block,)...  35.1 us
    pallas_call x1, Pallas kernels, attend_back(): pl.pallas_call(partial(attend_back_kernel, rows), grid=(seqs,), in_specs=...  24 us
    pallas_call x1, Pallas kernels, attend(): pl.pallas_call(partial(attend_kernel, rows), grid=(seqs,), in_specs=[per_...  16.4 us
    unnamed x38, local copies, waits for them, and re-layouts  16.1 us
    slice x1, local copies, waits for them, and re-layouts, body(): up_blocks[:, :, i]  13.1 us
  transfers between devices with their start and end apart: 6, of which 5 were waited for; matrix products, arithmetic and copies ran while one was open for 6% of the time, Pallas kernels for 9%

profile of v1, /device:TPU:0, one launch (start us, length us, event | category | flops | bytes accessed | tf_op | source)
XLA Modules:
  0.0 440.2 jit_solution(9820205941521420898)
XLA Ops:
  8.7 1.7 pad_maximum_fusion.1
  10.5 0.9 slice_dynamic-update-slice_fusion.3
  14.0 1.0 constant_dynamic-update-slice_fusion
  16.0 1.0 copy.39
  17.0 1.0 copy.24.live_ref
  18.0 49.6 %all-gather.5.cloned.1.call-done = bf16[3200,768]{1,0:T(8,128)(2,1)} async-done(((bf16[200,768]{1,0:T(8,128)(2,1)}), bf16[3200,768]{1,0:T(8,128)(2,1)}) %all-gather.5.cloned.1.call-update) | async-done | bytes 4915216 | tf_op jit(solution)/shard_map/all_gather | solution.py:331
  67.6 0.9 slice.110
  70.1 16.4 %attend.1 = (bf16[4,256,768]{2,1,0:T(8,128)(2,1)}, bf16[4,256,768]{2,1,0:T(8,128)(2,1)}, bf16[4,256,768]{2,1,0:T(8,128)(2,1)}, f32[4,6,256,512]{3,2,1,0:T(8,128)...) custom-call(bf16[4,256,768]{2,1,0:T(8,128)(2,1)} %x_ref.1, f32[4,256,1]{2,1,0:T(8,128)} %copy.24.live_ref, ...), custom_call_target="tpu_custom_call" | custom-call | tf_op jit(solution)/shard_map/attend/pallas_call | solution.py:232
  86.5 63.4 %all-gather.7.cloned.1.call-done = bf16[6144,768]{1,0:T(8,128)(2,1)} async-done(((bf16[384,768]{1,0:T(8,128)(2,1)}), bf16[6144,768]{1,0:T(8,128)(2,1)}) %all-gather.7.cloned.1.call-update) | async-done | bytes 9437200 | tf_op jit(solution)/shard_map/all_gather | solution.py:336
  149.9 35.1 %feed.1 = (bf16[1024,768]{1,0:T(8,128)(2,1)}, bf16[1024,3072]{1,0:T(8,128)(2,1)}, bf16[1024,3072]{1,0:T(8,128)(2,1)}, bf16[1024,768]{1,0:T(8,128)(2,1)}, bf16[10...) custom-call(f32[1024,768]{1,0:T(8,128)} %bitcast.73, ...), custom_call_target="tpu_custom_call" | custom-call | tf_op jit(solution)/shard_map/feed/pallas_call | solution.py:252
  185.0 9.1 %convolution_convert_fusion.1 = bf16[768,3072]{1,0:T(8,128)(2,1)} fusion(bf16[1024,768]{1,0:T(8,128)(2,1)} %get-tuple-element.40, bf16[1024,3072]{1,0:T(8,128)(2,1)} %get-tuple-element.41), kind=kOutput, calls=%fused_computation.2 | convolution fusion | flops 4834197504 | bytes 12582912 | tf_op jit(solution)/shard_map/dot_general | solution.py:368
  194.2 9.9 %reshape.126 = bf16[16,48,4,768]{3,2,1,0:T(4,128)(2,1)} reshape(bf16[768,3072]{1,0:T(8,128)(2,1)} %convolution_convert_fusion.1) | data formatting | bytes 9437184 | tf_op jit(solution)/shard_map/reshape | solution.py:369
  204.1 13.1 %fusion.11 = (bf16[16,48,1,768]{3,2,1,0:T(2,128)(2,1)S(1)}, bf16[16,48,1,768]{3,2,1,0:T(2,128)(2,1)S(1)}, bf16[16,48,1,768]{3,2,1,0:T(2,128)(2,1)S(1)}, bf16[16,48,1,768]{3,2,1,0:T(2,128)(2,1)S(1)}) fusion(bf16[16,48,4,768]{3,2,1,0:T(4,128)(2,1)} %reshape.126), kind=kLoop, calls=%fused_computation.46 | loop fusion | bytes 9437184 | tf_op jit(solution)/shard_map/slice | solution.py:372
  217.2 1.2 fusion.4
  219.1 5.5 %convolution_convert_fusion = bf16[3072,768]{1,0:T(8,128)(2,1)S(1)} fusion(bf16[1024,3072]{1,0:T(8,128)(2,1)S(1)} %bitcast.91, bf16[1024,768]{1,0:T(8,128)(2,1)S(1)} %copy-done.8), kind=kOutput, calls=%fused_computation.1 | convolution fusion | flops 4834197504 | bytes 12582912 | tf_op jit(solution)/shard_map/dot_general | solution.py:367
  224.6 1.2 fusion.3
  225.8 1.2 fusion.2
  227.0 1.2 fusion.1
  228.3 2.6 constant_dynamic-update-slice_fusion.6
  231.0 24.0 %attend_back.1 = (bf16[4,256,2304]{2,1,0:T(8,128)(2,1)}, bf16[4,256,768]{2,1,0:T(8,128)(2,1)}, f32[8,768]{1,0:T(8,128)}) custom-call(bf16[4,256,768]{2,1,0:T(8,128)(2,1)} %bitcast.75, bf16[16,200,768]{2,1,0:T(8,128)(2,1)} %bitcast.67, bf16[4,256,768]{2,1,0:T(8,128)(2,1)} %get-tuple-element.30.q_ref, bf16[4,256,768]{2,1,0:T(8,128)(2,1)} %get-tuple-element.31.k_ref, ...), custom_call_target="tpu_custom_call" | custom-call | tf_op jit(solution)/shard_map/attend_back/pallas_call | solution.py:279
  256.2 6.5 %fusion = bf16[768,2304]{1,0:T(8,128)(2,1)S(1)} fusion(bf16[4,256,2304]{2,1,0:T(8,128)(2,1)} %get-tuple-element.35, bf16[4,256,768]{2,1,0:T(8,128)(2,1)S(1)} %copy-done.1), kind=kOutput, calls=%fused_computation.3 | convolution fusion | flops 3625648128 | bytes 9830400 | tf_op jit(solution)/shard_map/dot_general | solution.py:383
  262.9 1.2 constant_dynamic-update-slice_fusion.5
  264.1 1.1 constant_dynamic-update-slice_fusion.4
  265.2 1.1 constant_dynamic-update-slice_fusion.3
  266.8 1.4 convolution_convert_fusion.2
  268.3 1.1 constant_dynamic-update-slice_fusion.2
  270.2 70.6 %reduce-scatter.5.cloned.1.call-done = bf16[1,384,768]{2,1,0:T(8,128)(2,1)} async-done(((bf16[16,384,768]{2,1,0:T(8,128)(2,1)}), bf16[1,384,768]{2,1,0:T(8,128)(2,1)}) %reduce-scatter.5.cloned.1.call-update) | async-done | bytes 589840 | tf_op jit(solution)/shard_map/reduce_scatter | solution.py:297
  340.8 1.5 collective-permute-start.1
  342.2 77.9 %reduce-scatter.3.cloned.1.call-done = bf16[1,200,768]{2,1,0:T(8,128)(2,1)} async-done(((bf16[16,200,768]{2,1,0:T(8,128)(2,1)}), bf16[1,200,768]{2,1,0:T(8,128)(2,1)}) %reduce-scatter.3.cloned.1.call-update) | async-done | bytes 307216 | tf_op jit(solution)/shard_map/reduce_scatter | solution.py:297
  420.1 1.5 collective-permute-start
  421.6 6.4 %collective-permute-done = bf16[200,768]{1,0:T(8,128)(2,1)S(1)} collective-permute-done((bf16[200,768]{1,0:T(8,128)(2,1)}, bf16[200,768]{1,0:T(8,128)(2,1)S(1)}, u32[]{:S(2)}, u32[]{:S(2)}) %collective-permute-start) | collective-permute-done | bytes 307232 | tf_op jit(solution)/shard_map/ppermute | solution.py:299
  428.0 1.0 convert_add_fusion.1
  (70 shorter events, 14.5 us)
Async XLA Ops:
  7.2 8.8 %copy-start.6 = (s32[4,256]{1,0:T(4,128)S(1)}, s32[4,256]{1,0:T(4,128)}, u32[]{:S(2)}) copy-start(s32[4,256]{1,0:T(4,128)} %param.10) | copy-start | bytes 12292
  7.2 60.4 %all-gather.5.cloned.1.call-start = ((), (), s32[]{:S(2)}) async-start(), calls=%async_computation.4 | async-start | bytes 5222400 | tf_op jit(solution)/shard_map/all_gather | solution.py:331
  10.4 139.5 %all-gather.7.cloned.1.call-start = ((), (), s32[]{:S(2)}) async-start(), calls=%async_computation.5 | async-start | bytes 10027008 | tf_op jit(solution)/shard_map/all_gather | solution.py:336
  15.0 0.8 copy-start.2
  15.9 324.9 %reduce-scatter.5.cloned.1.call-start = ((), (), s32[]{:S(2)}) async-start(), calls=%async_computation.3 | async-start | bytes 10027008 | tf_op jit(solution)/shard_map/reduce_scatter | solution.py:297
  194.2 24.3 %slice-start = ((s8[6291456]{0:T(1024)(128)(4,1)}), s8[2097152]{0:T(1024)(128)(4,1)S(1)}, s32[]{:S(2)}) async-start(s8[6291456]{0:T(1024)(128)(4,1)} %bitcast.90), calls=%async_computation.6 | async-start | bytes 4194304
  204.1 14.4 %slice-start.1 = ((s8[6291456]{0:T(1024)(128)(4,1)}), s8[4194304]{0:T(1024)(128)(4,1)S(1)}, s32[]{:S(2)}) async-start(s8[6291456]{0:T(1024)(128)(4,1)} %bitcast.90), calls=%async_computation.7 | async-start | bytes 8388608
  217.2 1.8 copy-start.8
  230.9 189.2 %reduce-scatter.3.cloned.1.call-start = ((), (), s32[]{:S(2)}) async-start(), calls=%async_computation.2 | async-start | bytes 5222400 | tf_op jit(solution)/shard_map/reduce_scatter | solution.py:297
  231.0 24.8 %copy-start.4 = (f32[1,3072]{1,0:T(1,128)S(1)}, f32[1,3072]{1,0:T(1,128)}, u32[]{:S(2)}) copy-start(f32[1,3072]{1,0:T(1,128)} %get-tuple-element.39) | copy-start | bytes 36868
  231.0 24.9 %copy-start.5 = (f32[8,768]{1,0:T(8,128)S(1)}, f32[8,768]{1,0:T(8,128)}, u32[]{:S(2)}) copy-start(f32[8,768]{1,0:T(8,128)} %get-tuple-element.38) | copy-start | bytes 73732
  231.0 25.2 %copy-start.1 = (bf16[4,256,768]{2,1,0:T(8,128)(2,1)S(1)}, bf16[4,256,768]{2,1,0:T(8,128)(2,1)}, u32[]{:S(2)}) copy-start(bf16[4,256,768]{2,1,0:T(8,128)(2,1)} %x_ref.1) | copy-start | bytes 4718596
  264.1 2.2 copy-start
  264.1 2.7 copy-start.7
  340.7 91.0 %copy-start.3 = (bf16[1,384,768]{2,1,0:T(8,128)(2,1)S(1)}, bf16[1,384,768]{2,1,0:T(8,128)(2,1)}, u32[]{:S(2)}) copy-start(bf16[1,384,768]{2,1,0:T(8,128)(2,1)} %reduce-scatter.5.cloned.1.call-done) | copy-start | bytes 1769476
  340.8 91.0 %collective-permute-start.1 = (bf16[384,768]{1,0:T(8,128)(2,1)}, bf16[384,768]{1,0:T(8,128)(2,1)S(1)}, u32[]{:S(2)}, u32[]{:S(2)}) collective-permute-start(bf16[384,768]{1,0:T(8,128)(2,1)} %bitcast.81), channel_id=1, source_target_pairs={{0,1},{1,0},{2,3},{3,2},{4,5},{5,4},{6,7},{7,6},{8,9},{9,8},{10,11... | collective-permute-start | bytes 1769480 | tf_op jit(solution)/shard_map/ppermute | solution.py:299
  420.1 7.8 %collective-permute-start = (bf16[200,768]{1,0:T(8,128)(2,1)}, bf16[200,768]{1,0:T(8,128)(2,1)S(1)}, u32[]{:S(2)}, u32[]{:S(2)}) collective-permute-start(bf16[200,768]{1,0:T(8,128)(2,1)} %bitcast.83), channel_id=1, source_target_pairs={{0,1},{1,0},{2,3},{3,2},{4,5},{5,4},{6,7},{7,6},{8,9},{9,8},{10,11... | collective-permute-start | bytes 921608 | tf_op jit(solution)/shard_map/ppermute | solution.py:299
Sparse Core Ops, SparseCore 0:
  10.7 56.8 all-gather.4
  70.4 79.4 all-gather.6
  231.1 109.6 reduce-scatter.4
  344.6 75.4 reduce-scatter.2

commit v2 on v1

--- a/solution.py
+++ b/solution.py
@@ -293,6 +293,126 @@
     )(grad_first, weights, query, key, value, probs)
 
 
+def slab_kernel(lhs_ref, rhs_ref, *refs):
+    out_ref = refs[-1]
+    out_ref[...] = mm(lhs_ref[...], rhs_ref[...], TN).reshape(out_ref.shape).astype(BF16)
+
+
+def slab(lhs, rhs, packed, block, place, steps, lhs_moves):
+    count, width = lhs.shape[0], packed.shape[-1]
+    moving = pl.BlockSpec((count, width), lambda i: (0, i))
+    still = pl.BlockSpec((count, width), lambda i: (0, 0))
+    held = [] if isinstance(packed, jax.ShapeDtypeStruct) else [packed]
+    return pl.pallas_call(
+        slab_kernel,
+        grid=(steps,),
+        in_specs=[
+            moving if lhs_moves else still,
+            still if lhs_moves else moving,
+        ]
+        + [pl.BlockSpec(memory_space=pl.ANY)] * len(held),
+        out_specs=pl.BlockSpec(block + (width,), place),
+        out_shape=shaped(packed.shape, BF16),
+        input_output_aliases={2: 0} if held else {},
+        name="slab",
+    )(lhs, rhs, *held)
+
+
+def fan_kernel(rows, me_ref, x_ref, d_ref, small_ref, out_ref):
+    step = pl.program_id(0)
+    core, across, side = me_ref[0], me_ref[1], me_ref[2]
+    width = x_ref.shape[-1]
+    half = width // 2
+    product = mm(x_ref[...], d_ref[...], TN)
+    start = pl.multiple_of(step * rows, rows)
+    for shard in range(width // rows):
+        to_core, to_across, to_z = shard & 1, (shard >> 1) & 1, shard >> 2
+        block = product[shard * rows : (shard + 1) * rows].astype(BF16)
+        for to_side in range(2):
+            cols = slice(to_side * half, (to_side + 1) * half)
+            out_ref[
+                to_core ^ core, to_side ^ side, to_across ^ across, to_z, pl.ds(start, rows), :
+            ] = block[:, cols]
+
+    @pl.when(step == 0)
+    def _():
+        for shard in range(width // rows):
+            to_core, to_across, to_z = shard & 1, (shard >> 1) & 1, shard >> 2
+            for to_side in range(2):
+                cols = slice(to_side * half, (to_side + 1) * half)
+                out_ref[
+                    to_core ^ core,
+                    to_side ^ side,
+                    to_across ^ across,
+                    to_z,
+                    3 * rows : 3 * rows + SMALL_ROWS,
+                    :,
+                ] = small_ref[shard, :, cols]
+
+
+def fan(tokens, grads, small, rows, me):
+    count, width = tokens.shape
+    shards = width // rows
+    shape = (2, 2, 2, shards // 4, 3 * rows + SMALL_ROWS, width // 2)
+    return pl.pallas_call(
+        partial(fan_kernel, rows),
+        grid=(3,),
+        in_specs=[
+            pl.BlockSpec(memory_space=pltpu.SMEM),
+            pl.BlockSpec((count, width), lambda i: (0, 0)),
+            pl.BlockSpec((count, width), lambda i: (0, i)),
+            kept(small.shape),
+        ],
+        out_specs=kept(shape),
+        out_shape=shaped(shape, BF16),
+        name="fan",
+    )(me, tokens, grads, small)
+
+
+def plus(one, other):
+    return (one.astype(F32) + other.astype(F32)).astype(BF16)
+
+
+def stepwise(parts, z_now, side):
+    size = lax.axis_size("fsdp")
+    depth = size // 4
+    swap_core = [(i, i ^ 1) for i in range(size)]
+    swap_across = [(i, i ^ 2) for i in range(size)]
+    swap_side = [(0, 1), (1, 0)]
+    got = lax.ppermute(parts[1], "fsdp", swap_core)
+    cut = parts.shape[-2] // 16 * 8
+    one, two = slice(0, cut), slice(cut, None)
+
+    def kept_part(side_at, across_at, rows):
+        return plus(parts[0, side_at, across_at, :, rows], got[side_at, across_at, :, rows])
+
+    side_sent = jnp.stack([kept_part(1, i, one) for i in range(2)])
+    across_sent = jnp.stack([kept_part(i, 1, two) for i in range(2)])
+    side_got = lax.ppermute(side_sent, "rep", swap_side)
+    across_got = lax.ppermute(across_sent, "fsdp", swap_across)
+    one_sent = plus(kept_part(0, 1, one), side_got[1])
+    two_sent = plus(kept_part(1, 0, two), across_got[1])
+    one_got = lax.ppermute(one_sent, "fsdp", swap_across)
+    two_got = lax.ppermute(two_sent, "rep", swap_side)
+    lines = jnp.concatenate(
+        [
+            plus(plus(kept_part(0, 0, one), side_got[0]), one_got),
+            plus(plus(kept_part(0, 0, two), across_got[0]), two_got),
+        ],
+        axis=1,
+    )
+    total = lax.dynamic_index_in_dim(lines, z_now, 0, False).astype(F32)
+    for hop in range(1, depth):
+        sent = lax.dynamic_index_in_dim(lines, (z_now + hop) % depth, 0, False)
+        turn = [(i, (i + 4 * hop) % size) for i in range(size)]
+        total = total + lax.ppermute(sent, "fsdp", turn).astype(F32)
+    own = total.astype(BF16)
+    other = lax.ppermute(own, "rep", swap_side)
+    low = jnp.where(side == 0, own, other)
+    high = jnp.where(side == 0, other, own)
+    return jnp.concatenate([low, high], axis=1).astype(F32)
+
+
 def scattered(packed):
     own = lax.psum_scatter(packed, "fsdp", scatter_dimension=0, tiled=True)[0]
     if lax.axis_size("rep") == 2:
@@ -364,27 +484,35 @@
         vec_all,
         bias_all,
     )
-    grad_down = jnp.dot(active.T, grad_second, preferred_element_type=F32).astype(BF16)
-    grad_up = jnp.dot(normed.T, grad_hidden, preferred_element_type=F32).astype(BF16)
-    up_blocks = grad_up.reshape(fsdp_size, own_rows, folds, width)
-    ffn_parts = scattered(
-        jnp.concatenate(
-            [up_blocks[:, :, i] for i in range(folds)]
-            + [grad_down.reshape(fsdp_size, hidden_own, width)],
-            axis=1,
-        )
-    )
+    tile = max(width // hidden_own, 1)
+    packed_rows = folds * own_rows + hidden_own + own_rows
+    packed = shaped((fsdp_size, packed_rows, width), BF16)
+    packed = slab(
+        active,
+        grad_second,
+        packed,
+        (tile, hidden_own),
+        lambda i: (i, folds * own_rows // hidden_own, 0),
+        folds,
+        True,
+    )
+    packed = slab(
+        normed, grad_hidden, packed, (fsdp_size, own_rows), lambda i: (0, i, 0), folds, False
+    )
+    context = context.reshape(token_count, width)
+    packed = slab(
+        context,
+        grad_first,
+        packed,
+        (fsdp_size, own_rows),
+        lambda i: (0, packed_rows // own_rows - 1, 0),
+        1,
+        False,
+    )
+    ffn_parts = scattered(packed)
     grad_qkv, grad_input, attn_small = attend_back(
         grad_first.reshape(seq_count, slot_count, width), attn_all, attn_rows, query, key, value, probs
     )
-    grad_out = jnp.dot(
-        context.reshape(token_count, width).T, grad_first, preferred_element_type=F32
-    )
-    grad_stack = jnp.dot(
-        layer_input.reshape(token_count, width).T,
-        grad_qkv.reshape(token_count, 3 * width),
-        preferred_element_type=F32,
-    ).astype(BF16)
     grad_vectors = jnp.concatenate([attn_small[:2], ffn_small[:6]])
     small_grad = jnp.concatenate(
         [
@@ -396,28 +524,31 @@
     small_grad = jnp.pad(
         small_grad, ((0, 0), (0, SMALL_ROWS * width - small_grad.shape[1]))
     ).reshape(fsdp_size, SMALL_ROWS, width)
-    attn_parts = scattered(
-        jnp.concatenate(
-            [
-                grad_stack[:, i * width : (i + 1) * width].reshape(fsdp_size, own_rows, width)
-                for i in range(3)
-            ]
-            + [grad_out.astype(BF16).reshape(fsdp_size, own_rows, width), small_grad],
-            axis=1,
+    tokens = layer_input.reshape(token_count, width)
+    grad_qkv = grad_qkv.reshape(token_count, 3 * width)
+    if lax.axis_size("rep") == 2 and own_rows % 16 == 0:
+        me = lax.axis_index("fsdp")
+        side = lax.axis_index("rep")
+        place = jnp.stack([me & 1, (me >> 1) & 1, side]).astype(jnp.int32)
+        attn_parts = stepwise(fan(tokens, grad_qkv, small_grad, own_rows, place), me >> 2, side)
+    else:
+        packed = shaped((fsdp_size, 3 * own_rows, width), BF16)
+        packed = slab(
+            tokens, grad_qkv, packed, (fsdp_size, own_rows), lambda i: (0, i, 0), 3, False
         )
-    )
-    small_part = attn_parts[4 * own_rows :].reshape(-1)
+        attn_parts = scattered(jnp.concatenate([packed, small_grad], axis=1))
+    small_part = attn_parts[3 * own_rows :].reshape(-1)
     return (
         output.reshape(layer_input.shape),
         grad_input,
         attn_parts[: 3 * own_rows].reshape(3, own_rows, width),
-        attn_parts[3 * own_rows : 4 * own_rows],
+        ffn_parts[-own_rows:],
         small_part[:vec_count].reshape(-1, own_rows),
         jnp.concatenate(
             [ffn_parts[i * own_rows : (i + 1) * own_rows] for i in range(folds)], axis=1
         ),
         small_part[vec_count : vec_count + hidden_own],
-        ffn_parts[folds * own_rows :],
+        ffn_parts[folds * own_rows : folds * own_rows + hidden_own],
     )
 
 

time: 441 us -> 366 us (0.83)
  waiting for transfers between devices: 268 us -> 205 us
  local copies, waits for them, and re-layouts: 52.6 us -> 17.8 us
  Pallas kernels: 75.5 us -> 106 us
  matrix products: 22.6 us -> 0 us
  starting transfers between devices: 3.09 us -> 11.2 us
  other arithmetic: 4.46 us -> 11.2 us
    reduce_scatter x2 -> x1, waiting for transfers between devices: 149 us -> 53.8 us  [scattered(): own = lax.psum_scatter(packed, 'fsdp', scatter_dimension=0, tiled=True)[0]]
    ppermute x0 -> x9, waiting for transfers between devices: none -> 37.9 us  [the longest x1 16.8 us: stepwise(): other = lax.ppermute(own, 'rep', swap_side)]
    pallas_call x0 -> x4, Pallas kernels: none -> 30.9 us  [the longest x3 22.8 us: slab(): pl.pallas_call(slab_kernel, grid=(steps,), in_specs=[moving if lhs_moves...]
    dot_general x4 -> x0, matrix products: 22.6 us -> none  [the longest x1 9.15 us: body(): jnp.dot(normed.T, grad_hidden, preferred_element_type=F32).astype(BF16)]
    slice x5 -> x1, local copies, waits for them, and re-layouts: 14.9 us -> 0.85 us  [body(): ffn_parts[folds * own_rows:folds * own_rows + hidden_own]]
    reshape x2 -> x1, local copies, waits for them, and re-layouts: 9.91 us -> 0.01 us  [body(): small_part = attn_parts[3 * own_rows:].reshape(-1)]
    unnamed x38 -> x18, local copies, waits for them, and re-layouts: 16.1 us -> 6.25 us
    ppermute x0 -> x9, starting transfers between devices: none -> 9.61 us  [the longest x3 4.5 us: stepwise(): total = total + lax.ppermute(sent, 'fsdp', turn).astype(F32)]
  transfers between devices with their start and end apart: 6 -> 13, of which waited for: 5 -> 9; matrix products, arithmetic and copies ran while one was open for 6% -> 6% of each run, Pallas kernels for 9% -> 13%
where the time goes in v2:
time: 366 us; the launch traced here: 365 us
  waiting for transfers between devices  205 us (56%)
  Pallas kernels  106 us (29%)
  local copies, waits for them, and re-layouts  17.8 us (5%)
  between operations  14 us (4%)
  starting transfers between devices  11.2 us (3%)
  other arithmetic  11.2 us (3%)
    all_gather x1, waiting for transfers between devices, body(): ffn_all = lax.all_gather(ffn_own, 'fsdp', axis=0)  63.4 us
    reduce_scatter x1, waiting for transfers between devices, scattered(): own = lax.psum_scatter(packed, 'fsdp', scatter_dimension=0, tiled=True)[0]  53.8 us
    all_gather x1, waiting for transfers between devices, body(): attn_all = lax.all_gather(attn_own, 'fsdp', axis=0)  49.6 us
    pallas_call x1, Pallas kernels, feed(): pl.pallas_call(partial(feed_kernel, rows, hidden), grid=(count // block,)...  35.1 us
    pallas_call x1, Pallas kernels, attend_back(): pl.pallas_call(partial(attend_back_kernel, rows), grid=(seqs,), in_specs=...  23.7 us
    pallas_call x3, Pallas kernels, slab(): pl.pallas_call(slab_kernel, grid=(steps,), in_specs=[moving if lhs_moves...  22.8 us
    ppermute x1, waiting for transfers between devices, stepwise(): other = lax.ppermute(own, 'rep', swap_side)  16.8 us
    pallas_call x1, Pallas kernels, attend(): pl.pallas_call(partial(attend_kernel, rows), grid=(seqs,), in_specs=[per_...  16.4 us
  transfers between devices with their start and end apart: 13, of which 9 were waited for; matrix products, arithmetic and copies ran while one was open for 6% of the time, Pallas kernels for 13%

profile of v2, /device:TPU:0, one launch (start us, length us, event | category | flops | bytes accessed | tf_op | source)
XLA Modules:
  0.0 365.0 jit_solution(8421357122828716815)
XLA Ops:
  8.7 1.7 pad_maximum_fusion.3
  14.0 1.0 constant_dynamic-update-slice_fusion
  15.9 1.0 copy.22.live_ref
  17.0 1.0 copy.27
  18.0 49.6 %all-gather.5.cloned.1.call-done = bf16[3200,768]{1,0:T(8,128)(2,1)} async-done(((bf16[200,768]{1,0:T(8,128)(2,1)}), bf16[3200,768]{1,0:T(8,128)(2,1)}) %all-gather.5.cloned.1.call-update) | async-done | bytes 4915216 | tf_op jit(solution)/shard_map/all_gather | solution.py:451
  70.1 16.4 %attend.1 = (bf16[4,256,768]{2,1,0:T(8,128)(2,1)}, bf16[4,256,768]{2,1,0:T(8,128)(2,1)}, bf16[4,256,768]{2,1,0:T(8,128)(2,1)}, f32[4,6,256,512]{3,2,1,0:T(8,128)...) custom-call(bf16[4,256,768]{2,1,0:T(8,128)(2,1)} %x_ref.1, f32[4,256,1]{2,1,0:T(8,128)} %copy.22.live_ref, ...), custom_call_target="tpu_custom_call" | custom-call | tf_op jit(solution)/shard_map/attend/pallas_call | solution.py:232
  86.5 63.4 %all-gather.7.cloned.1.call-done = bf16[6144,768]{1,0:T(8,128)(2,1)} async-done(((bf16[384,768]{1,0:T(8,128)(2,1)}), bf16[6144,768]{1,0:T(8,128)(2,1)}) %all-gather.7.cloned.1.call-update) | async-done | bytes 9437200 | tf_op jit(solution)/shard_map/all_gather | solution.py:456
  149.9 35.1 %feed.1 = (bf16[1024,768]{1,0:T(8,128)(2,1)}, bf16[1024,3072]{1,0:T(8,128)(2,1)}, bf16[1024,3072]{1,0:T(8,128)(2,1)}, bf16[1024,768]{1,0:T(8,128)(2,1)}, bf16[10...) custom-call(f32[1024,768]{1,0:T(8,128)} %bitcast.151, ...), custom_call_target="tpu_custom_call" | custom-call | tf_op jit(solution)/shard_map/feed/pallas_call | solution.py:252
  185.0 9.2 %slab.3.refs_0_ = bf16[16,432,768]{2,1,0:T(8,128)(2,1)} custom-call(bf16[1024,3072]{1,0:T(8,128)(2,1)} %get-tuple-element.42.lhs_ref, bf16[1024,768]{1,0:T(8,128)(2,1)} %get-tuple-element.43.rhs_ref), custom_call_target="tpu_custom_call" | custom-call | tf_op jit(solution)/shard_map/slab/pallas_call | solution.py:306
  194.2 9.2 %slab.4.refs_0_ = bf16[16,432,768]{2,1,0:T(8,128)(2,1)} custom-call(bf16[1024,768]{1,0:T(8,128)(2,1)} %get-tuple-element.40.lhs_ref, bf16[1024,3072]{1,0:T(8,128)(2,1)} %get-tuple-element.41.rhs_ref, bf16[16,432,768]{2,1,0:T(8,128)(2,1)} %slab.3.refs_0_), custom_call_target="tpu_custom_call", output_to_operand_aliasing={{}: (2, {})} | custom-call | tf_op jit(solution)/shard_map/slab/pallas_call | solution.py:306
  203.4 4.4 %slab.5 = bf16[16,432,768]{2,1,0:T(8,128)(2,1)} custom-call(bf16[1024,768]{1,0:T(8,128)(2,1)} %bitcast.153, bf16[1024,768]{1,0:T(8,128)(2,1)} %get-tuple-element.29.rhs_ref, bf16[16,432,768]{2,1,0:T(8,128)(2,1)} %slab.4.refs_0_), custom_call_target="tpu_custom_call", output_to_operand_aliasing={{}: (2, {})} | custom-call | tf_op jit(solution)/shard_map/slab/pallas_call | solution.py:306
  208.7 23.7 %attend_back.1 = (bf16[4,256,2304]{2,1,0:T(8,128)(2,1)}, bf16[4,256,768]{2,1,0:T(8,128)(2,1)}, f32[8,768]{1,0:T(8,128)}) custom-call(bf16[4,256,768]{2,1,0:T(8,128)(2,1)} %bitcast.148, bf16[16,200,768]{2,1,0:T(8,128)(2,1)} %bitcast.146, bf16[4,256,768]{2,1,0:T(8,128)(2,1)} %get-tuple-element.30.q_ref, bf16[4,256,768]{2,1,0:T(8,128)(2,1)} %get-tuple-element.31.k_ref, ...), custom_call_target="tpu_custom_call" | custom-call | tf_op jit(solution)/shard_map/attend_back/pallas_call | solution.py:279
  234.1 8.1 %fan.1 = bf16[2,2,2,4,152,384]{5,4,3,2,1,0:T(8,128)(2,1)} custom-call(s32[3]{0:T(128)} %pad_add_fusion.me_ref, bf16[1024,768]{1,0:T(8,128)(2,1)} %bitcast.149, bf16[1024,2304]{1,0:T(8,128)(2,1)} %bitcast.150, bf16[16,8,768]{2,1,0:T(8,128)(2,1)} %bitcast.157), custom_call_target="tpu_custom_call" | custom-call | tf_op jit(solution)/shard_map/fan/pallas_call | solution.py:357
  242.1 1.7 slice_bitcast_fusion
  244.1 3.6 collective-permute-done
  247.7 1.2 fusion.10
  249.0 1.5 collective-permute-start.1
  250.5 1.2 fusion.4
  252.3 9.1 %collective-permute-done.1 = bf16[2,4,72,384]{3,2,1,0:T(8,128)(2,1)} collective-permute-done((bf16[2,4,72,384]{3,2,1,0:T(8,128)(2,1)S(1)}, bf16[2,4,72,384]{3,2,1,0:T(8,128)(2,1)}, u32[]{:S(2)}, u32[]{:S(2)}) %collective-permute-start.1) | collective-permute-done | bytes 442400 | tf_op jit(solution)/shard_map/ppermute | solution.py:391
  261.4 1.2 fusion.6
  263.1 3.5 collective-permute-done.3
  266.7 1.1 fusion
  267.7 1.5 collective-permute-start.4
  269.3 1.9 collective-permute-done.2
  271.1 1.2 add_convert_fusion.1
  272.3 3.0 collective-permute-done.4
  275.3 1.1 add_convert_fusion
  276.4 3.4 collective-permute-start.7
  279.8 1.1 collective-permute-start.5
  280.9 53.8 %reduce-scatter.2.cloned.1.call-done = bf16[1,432,768]{2,1,0:T(8,128)(2,1)} async-done(((bf16[16,432,768]{2,1,0:T(8,128)(2,1)}), bf16[1,432,768]{2,1,0:T(8,128)(2,1)}) %reduce-scatter.2.cloned.1.call-update) | async-done | bytes 663568 | tf_op jit(solution)/shard_map/reduce_scatter | solution.py:417
  334.7 1.5 collective-permute-start.9
  336.9 16.8 %collective-permute-done.8 = bf16[152,384]{1,0:T(8,128)(2,1)S(1)} collective-permute-done((bf16[152,384]{1,0:T(8,128)(2,1)S(1)}, bf16[152,384]{1,0:T(8,128)(2,1)S(1)}, u32[]{:S(2)}, u32[]{:S(2)}) %collective-permute-start.8) | collective-permute-done | bytes 116768 | tf_op jit(solution)/shard_map/ppermute | solution.py:410
  (69 shorter events, 18.0 us)
Async XLA Ops:
  7.2 8.8 %copy-start.4 = (s32[4,256]{1,0:T(4,128)S(1)}, s32[4,256]{1,0:T(4,128)}, u32[]{:S(2)}) copy-start(s32[4,256]{1,0:T(4,128)} %param.10) | copy-start | bytes 12292
  7.2 60.4 %all-gather.5.cloned.1.call-start = ((), (), s32[]{:S(2)}) async-start(), calls=%async_computation.2 | async-start | bytes 5222400 | tf_op jit(solution)/shard_map/all_gather | solution.py:451
  10.4 139.5 %all-gather.7.cloned.1.call-start = ((), (), s32[]{:S(2)}) async-start(), calls=%async_computation.3 | async-start | bytes 10027008 | tf_op jit(solution)/shard_map/all_gather | solution.py:456
  15.0 0.8 copy-start
  15.9 318.9 %reduce-scatter.2.cloned.1.call-start = ((), (), s32[]{:S(2)}) async-start(), calls=%async_computation.1 | async-start | bytes 11280384 | tf_op jit(solution)/shard_map/reduce_scatter | solution.py:417
  207.8 0.7 copy-start.2
  207.8 0.8 copy-start.3
  243.8 3.9 %collective-permute-start = (bf16[2,2,4,152,384]{4,3,2,1,0:T(8,128)(2,1)S(1)}, bf16[2,2,4,152,384]{4,3,2,1,0:T(8,128)(2,1)S(1)}, u32[]{:S(2)}, u32[]{:S(2)}) collective-permute-start(bf16[2,2,4,152,384]{4,3,2,1,0:T(8,128)(2,1)S(1)} %slice_bitcast_fusion), channel_id=1, source_target_pairs={{0,2},{2,0},{4,6},{6,4},{8,10},{10,8},{12,14},{14,12},{16,18},{18,... | collective-permute-start | bytes 5603336 | tf_op jit(solution)/shard_map/ppermute | solution.py:382
  249.0 12.5 %collective-permute-start.1 = (bf16[2,4,72,384]{3,2,1,0:T(8,128)(2,1)S(1)}, bf16[2,4,72,384]{3,2,1,0:T(8,128)(2,1)}, u32[]{:S(2)}, u32[]{:S(2)}) collective-permute-start(bf16[2,4,72,384]{3,2,1,0:T(8,128)(2,1)S(1)} %pad_maximum_fusion.2), channel_id=1, source_target_pairs={{0,1},{1,0},{2,3},{3,2},{4,5},{5,4},{6,7},{7,6},{8,9},{9,8},{10,11... | collective-permute-start | bytes 1327112 | tf_op jit(solution)/shard_map/ppermute | solution.py:391
  251.7 14.9 %collective-permute-start.3 = (bf16[2,4,80,384]{3,2,1,0:T(8,128)(2,1)S(1)}, bf16[2,4,80,384]{3,2,1,0:T(8,128)(2,1)S(1)}, u32[]{:S(2)}, u32[]{:S(2)}) collective-permute-start(bf16[2,4,80,384]{3,2,1,0:T(8,128)(2,1)S(1)} %pad_maximum_fusion.1), channel_id=1, source_target_pairs={{0,4},{2,6},{4,0},{6,2},{8,12},{10,14},{12,8},{14,10},{16,20},{18,... | collective-permute-start | bytes 1474568 | tf_op jit(solution)/shard_map/ppermute | solution.py:392
  262.6 8.5 %collective-permute-start.2 = (bf16[4,72,384]{2,1,0:T(8,128)(2,1)S(1)}, bf16[4,72,384]{2,1,0:T(8,128)(2,1)S(1)}, u32[]{:S(2)}, u32[]{:S(2)}) collective-permute-start(bf16[4,72,384]{2,1,0:T(8,128)(2,1)S(1)} %fusion.6), channel_id=1, source_target_pairs={{0,4},{2,6},{4,0},{6,2},{8,12},{10,14},{12,8},{14,10},{16,20},{18,... | collective-permute-start | bytes 663560 | tf_op jit(solution)/shard_map/ppermute | solution.py:395
  267.7 7.6 %collective-permute-start.4 = (bf16[4,80,384]{2,1,0:T(8,128)(2,1)S(1)}, bf16[4,80,384]{2,1,0:T(8,128)(2,1)S(1)}, u32[]{:S(2)}, u32[]{:S(2)}) collective-permute-start(bf16[4,80,384]{2,1,0:T(8,128)(2,1)S(1)} %fusion), channel_id=1, source_target_pairs={{0,1},{1,0},{2,3},{3,2},{4,5},{5,4},{6,7},{7,6},{8,9},{9,8},{10,11... | collective-permute-start | bytes 737288 | tf_op jit(solution)/shard_map/ppermute | solution.py:396
  276.4 59.7 %collective-permute-start.7 = (bf16[152,384]{1,0:T(8,128)(2,1)S(1)}, bf16[152,384]{1,0:T(8,128)(2,1)S(1)}, u32[]{:S(2)}, u32[]{:S(2)}) collective-permute-start(bf16[152,384]{1,0:T(8,128)(2,1)S(1)} %get-tuple-element.55), channel_id=1, source_target_pairs={{0,24},{2,26},{4,28},{6,30},{8,0},{10,2},{12,4},{14,6},{16,8},{18,... | collective-permute-start | bytes 350216 | tf_op jit(solution)/shard_map/ppermute | solution.py:408
  279.8 56.4 %collective-permute-start.6 = (bf16[152,384]{1,0:T(8,128)(2,1)S(1)}, bf16[152,384]{1,0:T(8,128)(2,1)S(1)}, u32[]{:S(2)}, u32[]{:S(2)}) collective-permute-start(bf16[152,384]{1,0:T(8,128)(2,1)S(1)} %get-tuple-element.54), channel_id=1, source_target_pairs={{0,16},{2,18},{4,20},{6,22},{8,24},{10,26},{12,28},{14,30},{16,0},... | collective-permute-start | bytes 350216 | tf_op jit(solution)/shard_map/ppermute | solution.py:408
  279.8 56.4 %collective-permute-start.5 = (bf16[152,384]{1,0:T(8,128)(2,1)S(1)}, bf16[152,384]{1,0:T(8,128)(2,1)S(1)}, u32[]{:S(2)}, u32[]{:S(2)}) collective-permute-start(bf16[152,384]{1,0:T(8,128)(2,1)S(1)} %get-tuple-element.53), channel_id=1, source_target_pairs={{0,8},{2,10},{4,12},{6,14},{8,16},{10,18},{12,20},{14,22},{16,24},... | collective-permute-start | bytes 350216 | tf_op jit(solution)/shard_map/ppermute | solution.py:408
  334.7 21.1 %copy-start.1 = (bf16[1,432,768]{2,1,0:T(8,128)(2,1)S(1)}, bf16[1,432,768]{2,1,0:T(8,128)(2,1)}, u32[]{:S(2)}) copy-start(bf16[1,432,768]{2,1,0:T(8,128)(2,1)} %reduce-scatter.2.cloned.1.call-done) | copy-start | bytes 1990660
  334.7 21.1 %collective-permute-start.9 = (bf16[432,768]{1,0:T(8,128)(2,1)}, bf16[432,768]{1,0:T(8,128)(2,1)S(1)}, u32[]{:S(2)}, u32[]{:S(2)}) collective-permute-start(bf16[432,768]{1,0:T(8,128)(2,1)} %bitcast.158), channel_id=1, source_target_pairs={{0,1},{1,0},{2,3},{3,2},{4,5},{5,4},{6,7},{7,6},{8,9},{9,8},{10,11... | collective-permute-start | bytes 1990664 | tf_op jit(solution)/shard_map/ppermute | solution.py:419
  336.3 17.4 %collective-permute-start.8 = (bf16[152,384]{1,0:T(8,128)(2,1)S(1)}, bf16[152,384]{1,0:T(8,128)(2,1)S(1)}, u32[]{:S(2)}, u32[]{:S(2)}) collective-permute-start(bf16[152,384]{1,0:T(8,128)(2,1)S(1)} %fusion.16), channel_id=1, source_target_pairs={{0,1},{1,0},{2,3},{3,2},{4,5},{5,4},{6,7},{7,6},{8,9},{9,8},{10,11... | collective-permute-start | bytes 350216 | tf_op jit(solution)/shard_map/ppermute | solution.py:410
Sparse Core Ops, SparseCore 0:
  10.7 56.8 all-gather.4
  70.4 79.4 all-gather.6
  208.0 126.7 reduce-scatter.1
